TPU v7x, 32 devices: a whole 2x2x4 slice. The times are simulated.
32 devices in a mesh: groups: 2 (over y), tm: 4 (over z), space: 2 (over x), chan: 2 (over core).
Axes of the slice: x: 2, y: 2, z: 4, core: 2. Of those that a mesh axis runs over, the one named last changes fastest.
Arguments:
- latents: bfloat16 [8, 8, 160, 384], P(('groups', 'tm'), 'space', None, 'chan'), parts along dimension 0, may hold values from -30 to 30
- norm_gain: float32 [384], P('chan'), may hold values from 0.1 to 1.9
- conv_weight: bfloat16 [3, 3, 3, 384, 384], P(None, None, None, 'chan'), may hold values from -0.0625 to 0.0625
- conv_bias: float32 [384], P('chan'), may hold values from -2 to 2
- attention_gain: float32 [384], P('chan'), may hold values from 0.1 to 1.9
- qkv_weight: bfloat16 [384, 1152], P('chan'), may hold values from -3 to 3
- out_weight: bfloat16 [384, 384], replicated, may hold values from -0.3125 to 0.3125
Outputs:
- block_output: bfloat16 [8, 8, 160, 384], P(('groups', 'tm'), 'space', None, 'chan'), parts along dimension 0
There are 2 independent parts, one for each index of `groups`. A program takes and returns all parts, laid end to end along the dimension named above; an argument that names none is the same for every part. Nothing has to cross between parts.
All inputs are finite; a program needn't handle non-finite values.
Results may differ from a plain program's by a relative error of at most 0.019.
Values may be sent and summed in bfloat16 or wider, within the bound.
No kernel may reach another device: no remote copies, remote signals or barrier semaphores. Data moves between devices by JAX's collectives and lax.ppermute only.
A program may use at most 64 MiB of HBM per device.

v0:
```python
import math
import jax
import jax.numpy as jnp
from jax import lax
from jax.sharding import PartitionSpec as P

epsilon = 1e-06


def passed_along(shard, axis, by):
    peers = lax.axis_size(axis)
    pairs = [(i, i + by) for i in range(peers) if 0 <= i + by < peers]
    return lax.ppermute(shard, axis, pairs)


def extended(cells, sides, width):
    for axis, dim in sides:
        count = lax.axis_size(axis)
        ends = count - 1
        head = lax.slice_in_dim(cells, 0, width, axis=dim)
        tail = lax.slice_in_dim(cells, cells.shape[dim] - width, cells.shape[dim], axis=dim)
        cells = jnp.concatenate(
            [
                lax.ppermute(tail, axis, [(i, (i + 1) % count) for i in range(ends)]),
                cells,
                lax.ppermute(head, axis, [((i + 1) % count, i) for i in range(ends)]),
            ],
            axis=dim,
        )
    return cells


def attend_update(running, queries, key_rows, value_rows, score_scale):
    peak, total, summed = running
    scores = (
        lax.dot_general(
            queries, key_rows, (((1,), (1,)), ((), ())), preferred_element_type=jnp.float32
        )
        * score_scale
    )
    new_peak = jnp.maximum(peak, jnp.max(scores, axis=1))
    weights = jnp.exp(scores - new_peak[:, None])
    total = jnp.sum(weights, axis=1)
    summed = jnp.dot(weights.astype(jnp.bfloat16), value_rows, preferred_element_type=jnp.float32)
    return (new_peak, total, summed)


def shards(latents, norm_gain, conv_weight, conv_bias, attention_gain, qkv_weight, out_weight):
    row_count = latents.shape[1]
    col_count = latents.shape[2]
    half_chan = latents.shape[3]
    channels = conv_weight.shape[4]
    pos_count = row_count * col_count
    core_count = lax.axis_size("chan")
    own_rows = pos_count // core_count
    score_scale = 1.0 / math.sqrt(channels)
    input_float = latents[0].astype(jnp.float32)
    square_sums = lax.psum(jnp.sum(input_float * input_float, axis=-1), "chan")
    first = jax.nn.silu(
        input_float * lax.rsqrt(square_sums / channels + epsilon)[..., None] * norm_gain
    ).astype(jnp.bfloat16)
    previous = passed_along(first, "tm", 1)
    earlier = passed_along(first, "tm", 2)
    stacked = jnp.stack([earlier, previous, first])
    rimmed = extended(stacked, (("space", 1),), 1)
    padded = jnp.pad(rimmed, ((0, 0), (0, 0), (1, 1), (0, 0)))
    pieces = []
    for frame_off in range(3):
        for row_off in range(3):
            for col_off in range(3):
                pieces.append(
                    padded[
                        frame_off, row_off : row_off + row_count, col_off : col_off + col_count
                    ].reshape(pos_count, half_chan)
                )
    columns = jnp.concatenate(pieces, axis=1)
    flat_weight = conv_weight.reshape(27 * half_chan, channels)
    partial_value = jnp.dot(columns, flat_weight, preferred_element_type=jnp.float32)
    own_part = lax.psum_scatter(partial_value, "chan", scatter_dimension=1, tiled=True)
    stream_float = (
        (input_float.reshape(pos_count, half_chan) + own_part + conv_bias)
        .astype(jnp.bfloat16)
        .astype(jnp.float32)
    )
    stream_sums = lax.psum(jnp.sum(stream_float * stream_float, axis=-1), "chan")
    second = (
        stream_float * lax.rsqrt(stream_sums / channels + epsilon)[:, None] * attention_gain
    ).astype(jnp.bfloat16)
    initial = (
        jnp.full((own_rows,), -1e30, jnp.float32),
        jnp.zeros((own_rows,), jnp.float32),
        jnp.zeros((own_rows, channels), jnp.float32),
    )
    owned_inputs = lax.all_to_all(second, "chan", split_axis=0, concat_axis=1, tiled=True)
    owned_weights = lax.all_gather(qkv_weight, "chan", axis=0, tiled=True)
    own_qkv = jnp.dot(owned_inputs, owned_weights, preferred_element_type=jnp.float32).astype(
        jnp.bfloat16
    )
    own_queries = own_qkv[:, :channels]
    running = attend_update(
        initial,
        own_queries,
        lax.all_gather(own_qkv[:, channels : 2 * channels], ("space", "chan"), axis=0, tiled=True),
        lax.all_gather(own_qkv[:, 2 * channels :], ("space", "chan"), axis=0, tiled=True),
        score_scale,
    )
    attended = (running[2] / running[1][:, None]).astype(jnp.bfloat16)
    projected = jnp.dot(attended, out_weight, preferred_element_type=jnp.float32).astype(
        jnp.bfloat16
    )
    restored = lax.all_to_all(projected, "chan", split_axis=1, concat_axis=0, tiled=True)
    output = (stream_float + restored.astype(jnp.float32)).astype(jnp.bfloat16)
    return output.reshape(1, row_count, col_count, half_chan)


def solution(mesh):
    placed = (
        P(("groups", "tm"), "space", None, "chan"),
        P("chan"),
        P(None, None, None, "chan", None),
        P("chan"),
        P("chan"),
        P("chan", None),
        P(),
    )
    return jax.shard_map(
        shards,
        mesh=mesh,
        in_specs=placed,
        out_specs=P(("groups", "tm"), "space", None, "chan"),
        check_vma=False,
    )
```

profile of v0, /device:TPU:0, one launch (start us, length us, event | category | flops | bytes accessed | tf_op | source)
XLA Modules:
  0.0 130.4 jit_solution(6493389005145552808)
XLA Ops:
  6.5 0.0 copy-start
  6.5 0.0 reduce-scatter.2.cloned.1.call-start
  6.5 1.2 fusion.13
  7.8 2.6 %psum.14 = f32[4,160]{1,0:T(4,128)S(1)} all-reduce(f32[4,160]{1,0:T(4,128)S(1)} %fusion.13), channel_id=1, replica_groups=mesh['groups'=2,'tm'=4,'space'=2,'chan'=2] {'chan'}, use_global_device_ids=true, to_apply=%region_1.0 | all-reduce | flops 640 | bytes 5120 | tf_op jit(solution)/shard_map/psum | solution.py:58
  10.4 1.3 multiply_convert_fusion.1
  11.7 5.8 %collective-permute-start = (bf16[4,160,192]{2,1,0:T(8,128)(2,1)S(1)}, bf16[4,160,192]{2,1,0:T(8,128)(2,1)S(1)}, u32[]{:S(2)}, u32[]{:S(2)}) collective-permute-start(bf16[4,160,192]{2,1,0:T(8,128)(2,1)S(1)} %multiply_convert_fusion.1), channel_id=1, source_target_pairs={{0,8},{4,12},{1,9},{5,13},{2,10},{6,14},{3,11},{7,15},{16,24},{20,... | collective-permute-start | bytes 737288 | tf_op jit(solution)/shard_map/ppermute | solution.py:13
  17.5 3.5 %collective-permute-start.1 = (bf16[4,160,192]{2,1,0:T(8,128)(2,1)S(1)}, bf16[4,160,192]{2,1,0:T(8,128)(2,1)S(1)}, u32[]{:S(2)}, u32[]{:S(2)}) collective-permute-start(bf16[4,160,192]{2,1,0:T(8,128)(2,1)S(1)} %multiply_convert_fusion.1), channel_id=1, source_target_pairs={{0,4},{4,8},{8,12},{1,5},{5,9},{9,13},{2,6},{6,10},{10,14},{3,7},{... | collective-permute-start | bytes 737288 | tf_op jit(solution)/shard_map/ppermute | solution.py:13
  21.0 1.3 multiply_convert_fusion
  22.3 3.3 %collective-permute-done = bf16[4,160,192]{2,1,0:T(8,128)(2,1)S(1)} collective-permute-done((bf16[4,160,192]{2,1,0:T(8,128)(2,1)S(1)}, bf16[4,160,192]{2,1,0:T(8,128)(2,1)S(1)}, u32[]{:S(2)}, u32[]{:S(2)}) %collective-permute-start) | collective-permute-done | bytes 245792 | tf_op jit(solution)/shard_map/ppermute | solution.py:13
  25.6 6.2 %collective-permute-done.1 = bf16[4,160,192]{2,1,0:T(8,128)(2,1)S(1)} collective-permute-done((bf16[4,160,192]{2,1,0:T(8,128)(2,1)S(1)}, bf16[4,160,192]{2,1,0:T(8,128)(2,1)S(1)}, u32[]{:S(2)}, u32[]{:S(2)}) %collective-permute-start.1) | collective-permute-done | bytes 245792 | tf_op jit(solution)/shard_map/ppermute | solution.py:13
  31.9 0.1 pad_maximum_fusion.12
  32.0 3.4 %collective-permute-start.2 = (bf16[3,1,160,192]{3,2,1,0:T(8,128)(2,1)S(1)}, bf16[3,1,160,192]{3,2,1,0:T(8,128)(2,1)S(1)}, u32[]{:S(2)}, u32[]{:S(2)}) collective-permute-start(bf16[3,1,160,192]{3,2,1,0:T(8,128)(2,1)S(1)} %get-tuple-element.31), channel_id=1, source_target_pairs={{0,2},{1,3},{4,6},{5,7},{8,10},{9,11},{12,14},{13,15},{16,18},{17,... | collective-permute-start | bytes 552968 | tf_op jit(solution)/shard_map/ppermute | solution.py:24
  35.4 1.3 collective-permute-start.3
  36.7 3.4 %collective-permute-done.2 = bf16[3,1,160,192]{3,2,1,0:T(8,128)(2,1)S(1)} collective-permute-done((bf16[3,1,160,192]{3,2,1,0:T(8,128)(2,1)S(1)}, bf16[3,1,160,192]{3,2,1,0:T(8,128)(2,1)S(1)}, u32[]{:S(2)}, u32[]{:S(2)}) %collective-permute-start.2) | collective-permute-done | bytes 184352 | tf_op jit(solution)/shard_map/ppermute | solution.py:24
  40.0 4.1 %collective-permute-done.3 = bf16[3,1,160,192]{3,2,1,0:T(8,128)(2,1)S(1)} collective-permute-done((bf16[3,1,160,192]{3,2,1,0:T(8,128)(2,1)S(1)}, bf16[3,1,160,192]{3,2,1,0:T(8,128)(2,1)S(1)}, u32[]{:S(2)}, u32[]{:S(2)}) %collective-permute-start.3) | collective-permute-done | bytes 184352 | tf_op jit(solution)/shard_map/ppermute | solution.py:26
  44.2 0.7 select_maximum_fusion
  44.9 2.3 %fusion.21 = (bf16[1,4,160,192]{3,2,1,0:T(8,128)(2,1)S(1)}, bf16[1,4,160,192]{3,2,1,0:T(8,128)(2,1)S(1)}, bf16[1,4,160,192]{3,2,1,0:T(8,128)(2,1)S(1)}, bf16[1,4...) fusion(bf16[3,6,162,192]{3,2,1,0:T(8,128)(2,1)S(1)} %select_max, ...), kind=kLoop, calls=%fused_computation.52 | loop fusion | bytes 8847360 | tf_op jit(solution)/shard_map/slice | solution.py:72
  47.2 1.1 pad_maximum_fusion
  48.3 1.0 pad_maximum_fusion.3
  49.3 11.7 %concatenate.19 = bf16[640,5184]{1,0:T(8,128)(2,1)} concatenate(bf16[640,192]{1,0:T(8,128)(2,1)} %bitcast.88, bf16[640,192]{1,0:T(8,128)(2,1)} %bitcast.93, bf16[640,192]{1,0:T(8,128)(2,1)} %bitcast.87, bf16[640,192]{1,0:T(8,128)(2,1)} %bitcast.86, bf16[640,192]{1,0:T(8,128)(2,1)S(1)} %bitcast.64, bf16[640,192]{1,0:T(8,128)(2,1)} %bitcast.85, bf16[640,192]{1,0:T(8,128)(2,1)} %bitcast.84, ...), dimensions={1} | concatenate | bytes 13271040 | tf_op jit(solution)/shard_map/concatenate | solution.py:76
  61.1 0.0 copy-start.1
  61.1 8.4 %fusion.24 = f32[640,384]{0,1:T(8,128)} fusion(bf16[640,5184]{1,0:T(8,128)(2,1)} %concatenate.19, bf16[5184,384]{1,0:T(8,128)(2,1)} %bitcast.97), kind=kOutput, calls=%fused_computation.55 | convolution fusion | flops 2548039680 | bytes 11599872 | tf_op jit(solution)/shard_map/dot_general | solution.py:78
  69.5 0.0 reduce-scatter.2.cloned.1.call-update
  69.5 0.0 copy-done.1
  69.5 0.0 copy-start.4
  69.6 0.2 copy.11
  69.7 0.8 copy-done.3
  70.5 2.4 %all_gather.9 = bf16[384,1152]{1,0:T(8,128)(2,1)S(1)} all-gather(bf16[192,1152]{1,0:T(8,128)(2,1)S(1)} %copy-done.3), channel_id=1, replica_groups=mesh['groups'=2,'tm'=4,'space'=2,'chan'=2] {'chan'}, dimensions={0}, use_global_device_ids=true | all-gather | bytes 1327104 | tf_op jit(solution)/shard_map/all_gather | solution.py:95
  72.9 12.9 %reduce-scatter.2.cloned.1.call-done = f32[640,192]{0,1:T(8,128)} async-done(((f32[640,384]{0,1:T(8,128)}), f32[640,192]{0,1:T(8,128)}) %reduce-scatter.2.cloned.1.call-update) | async-done | bytes 491536 | tf_op jit(solution)/shard_map/reduce_scatter | solution.py:79
  85.9 0.0 copy-done.5
  85.9 1.2 fusion.15
  87.0 2.5 %psum.15 = f32[640]{0:T(1024)S(1)} all-reduce(f32[640]{0:T(1024)S(1)} %get-tuple-element.5), channel_id=1, replica_groups=mesh['groups'=2,'tm'=4,'space'=2,'chan'=2] {'chan'}, use_global_device_ids=true, to_apply=%region_4.5 | all-reduce | flops 640 | bytes 5120 | tf_op jit(solution)/shard_map/psum | solution.py:85
  89.5 0.1 fusion.17
  89.6 0.3 all_to_all.24
  89.9 4.0 %all_to_all.32 = bf16[2,320,192]{1,2,0:T(8,128)(2,1)S(1)} all-to-all(bf16[2,320,192]{1,2,0:T(8,128)(2,1)S(1)} %copy.12), channel_id=1, replica_groups=mesh['groups'=2,'tm'=4,'space'=2,'chan'=2] {'chan'}, dimensions={0} | all-to-all | bytes 491520 | tf_op jit(solution)/shard_map/all_to_all | solution.py:94
  93.9 0.6 convolution_convert_fusion
  94.5 0.1 fusion.22
  94.6 9.9 %all_gather.10 = bf16[1280,384]{1,0:T(8,128)(2,1)S(1)} all-gather(bf16[320,384]{1,0:T(8,128)(2,1)S(1)} %get-tuple-element.33), channel_id=1, replica_groups=mesh['groups'=2,'tm'=4,'space'=2,'chan'=2] {'space','chan'}, dimensions={0}, use_global_device_ids=true | all-gather | bytes 1228800 | tf_op jit(solution)/shard_map/all_gather | solution.py:103
  104.5 0.7 fusion.23
  105.2 10.2 %all_gather.11 = bf16[1280,384]{1,0:T(8,128)(2,1)} all-gather(bf16[320,384]{1,0:T(8,128)(2,1)S(1)} %get-tuple-element.34), channel_id=1, replica_groups=mesh['groups'=2,'tm'=4,'space'=2,'chan'=2] {'space','chan'}, dimensions={0}, use_global_device_ids=true | all-gather | bytes 1228800 | tf_op jit(solution)/shard_map/all_gather | solution.py:104
  115.4 0.4 fusion.6
  115.8 0.8 copy-done.2
  116.6 0.9 convolution_convert_fusion.1
  117.5 0.2 copy.13
  117.7 4.0 %all_to_all.33 = bf16[320,2,192]{0,2,1:T(8,128)(2,1)S(1)} all-to-all(bf16[320,2,192]{0,2,1:T(8,128)(2,1)S(1)} %bitcast.95), channel_id=1, replica_groups=mesh['groups'=2,'tm'=4,'space'=2,'chan'=2] {'chan'}, dimensions={1} | all-to-all | bytes 491520 | tf_op jit(solution)/shard_map/all_to_all | solution.py:111
  121.7 0.5 copy.14
  122.2 0.4 reshape.35
  122.6 0.9 copy.15
  (11 shorter events, 0.2 us)
Async XLA Ops:
  6.5 109.3 %copy-start = (bf16[384,384]{1,0:T(8,128)(2,1)S(1)}, bf16[384,384]{1,0:T(8,128)(2,1)}, u32[]{:S(2)}) copy-start(bf16[384,384]{1,0:T(8,128)(2,1)} %param.13) | copy-start | bytes 884740
  6.5 79.3 %reduce-scatter.2.cloned.1.call-start = ((), (), s32[]{:S(2)}) async-start(), calls=%async_computation.3 | async-start | bytes 1474560 | tf_op jit(solution)/shard_map/reduce_scatter | solution.py:79
  11.7 13.9 %collective-permute-start = (bf16[4,160,192]{2,1,0:T(8,128)(2,1)S(1)}, bf16[4,160,192]{2,1,0:T(8,128)(2,1)S(1)}, u32[]{:S(2)}, u32[]{:S(2)}) collective-permute-start(bf16[4,160,192]{2,1,0:T(8,128)(2,1)S(1)} %multiply_convert_fusion.1), channel_id=1, source_target_pairs={{0,8},{4,12},{1,9},{5,13},{2,10},{6,14},{3,11},{7,15},{16,24},{20,... | collective-permute-start | bytes 737288 | tf_op jit(solution)/shard_map/ppermute | solution.py:13
  17.5 14.3 %collective-permute-start.1 = (bf16[4,160,192]{2,1,0:T(8,128)(2,1)S(1)}, bf16[4,160,192]{2,1,0:T(8,128)(2,1)S(1)}, u32[]{:S(2)}, u32[]{:S(2)}) collective-permute-start(bf16[4,160,192]{2,1,0:T(8,128)(2,1)S(1)} %multiply_convert_fusion.1), channel_id=1, source_target_pairs={{0,4},{4,8},{8,12},{1,5},{5,9},{9,13},{2,6},{6,10},{10,14},{3,7},{... | collective-permute-start | bytes 737288 | tf_op jit(solution)/shard_map/ppermute | solution.py:13
  32.0 8.1 %collective-permute-start.2 = (bf16[3,1,160,192]{3,2,1,0:T(8,128)(2,1)S(1)}, bf16[3,1,160,192]{3,2,1,0:T(8,128)(2,1)S(1)}, u32[]{:S(2)}, u32[]{:S(2)}) collective-permute-start(bf16[3,1,160,192]{3,2,1,0:T(8,128)(2,1)S(1)} %get-tuple-element.31), channel_id=1, source_target_pairs={{0,2},{1,3},{4,6},{5,7},{8,10},{9,11},{12,14},{13,15},{16,18},{17,... | collective-permute-start | bytes 552968 | tf_op jit(solution)/shard_map/ppermute | solution.py:24
  35.4 8.8 %collective-permute-start.3 = (bf16[3,1,160,192]{3,2,1,0:T(8,128)(2,1)S(1)}, bf16[3,1,160,192]{3,2,1,0:T(8,128)(2,1)S(1)}, u32[]{:S(2)}, u32[]{:S(2)}) collective-permute-start(bf16[3,1,160,192]{3,2,1,0:T(8,128)(2,1)S(1)} %get-tuple-element.32), channel_id=1, source_target_pairs={{2,0},{3,1},{6,4},{7,5},{10,8},{11,9},{14,12},{15,13},{18,16},{19,... | collective-permute-start | bytes 552968 | tf_op jit(solution)/shard_map/ppermute | solution.py:26
  61.1 8.5 %copy-start.1 = (bf16[1,4,160,192]{3,2,1,0:T(8,128)(2,1)S(1)}, bf16[1,4,160,192]{3,2,1,0:T(8,128)(2,1)}, u32[]{:S(2)}) copy-start(bf16[1,4,160,192]{3,2,1,0:T(8,128)(2,1)} %param.7) | copy-start | bytes 737284
  69.5 1.0 copy-start.3
  69.5 16.4 %copy-start.5 = (f32[192]{0:T(256)S(1)}, f32[192]{0:T(256)}, u32[]{:S(2)}) copy-start(f32[192]{0:T(256)} %param.10) | copy-start | bytes 2308
  69.5 20.0 %copy-start.4 = (f32[192]{0:T(256)S(1)}, f32[192]{0:T(256)}, u32[]{:S(2)}) copy-start(f32[192]{0:T(256)} %param.11) | copy-start | bytes 2308
  115.4 1.2 copy-start.2
Sparse Core Ops, SparseCore 0:
  69.7 16.1 reduce-scatter.1
where the time goes:
time: 132 us; the launch traced here: 130 us
  blocking collectives  35.6 us (27%)
  waiting for transfers between devices  30 us (23%)
  local copies, waits for them, and re-layouts  18.1 us (14%)
  starting transfers between devices  14 us (11%)
  between operations  13.6 us (10%)
  matrix products  10.6 us (8%)
  other arithmetic  8.47 us (6%)
    reduce_scatter x1, waiting for transfers between devices, shards(): lax.psum_scatter(partial_value, 'chan', scatter_dimension=1, tiled=True)  12.9 us
    concatenate x1, local copies, waits for them, and re-layouts, shards(): columns = jnp.concatenate(pieces, axis=1)  11.7 us
    all_gather x1, blocking collectives, shards(): lax.all_gather(own_qkv[:, 2 * channels:], ('space', 'chan'), axis=0, tile...  10.2 us
    all_gather x1, blocking collectives, shards(): lax.all_gather(own_qkv[:, channels:2 * channels], ('space', 'chan'), axis...  9.93 us
    ppermute x2, waiting for transfers between devices, passed_along(): return lax.ppermute(shard, axis, pairs)  9.56 us
    ppermute x2, starting transfers between devices, passed_along(): return lax.ppermute(shard, axis, pairs)  9.33 us
    dot_general x1, matrix products, shards(): jnp.dot(columns, flat_weight, preferred_element_type=jnp.float32)  8.42 us
    ppermute x1, waiting for transfers between devices, extended(): lax.ppermute(head, axis, [((i + 1) % count, i) for i in range(ends)])  4.13 us
  transfers between devices with their start and end apart: 5, of which 5 were waited for; matrix products, arithmetic and copies ran while one was open for 1% of the time, Pallas kernels for 0%

commit v1 on v0

--- a/solution.py
+++ b/solution.py
@@ -5,6 +5,11 @@
 from jax.sharding import PartitionSpec as P
 
 epsilon = 1e-06
+
+
+def all_by_exchange(array, axis, d):
+    sent = jnp.stack([array] * lax.axis_size(axis))
+    return jnp.concatenate(lax.all_to_all(sent, axis, 0, 0), axis=d)
 
 
 def passed_along(shard, axis, by):
@@ -101,7 +106,7 @@
         initial,
         own_queries,
         lax.all_gather(own_qkv[:, channels : 2 * channels], ("space", "chan"), axis=0, tiled=True),
-        lax.all_gather(own_qkv[:, 2 * channels :], ("space", "chan"), axis=0, tiled=True),
+        all_by_exchange(own_qkv[:, 2 * channels :], ("space", "chan"), 0),
         score_scale,
     )
     attended = (running[2] / running[1][:, None]).astype(jnp.bfloat16)

time: 132 us -> 139 us (1.053)
  starting transfers between devices: 14 us -> 18.3 us
  matrix products: 10.6 us -> 12.7 us
    all_gather x1 -> x0, blocking collectives: 10.2 us -> none  [shards(): lax.all_gather(own_qkv[:, 2 * channels:], ('space', 'chan'), axis=0, tile...]
    all_gather x1, blocking collectives: 9.93 us -> 19.9 us  [shards(): lax.all_gather(own_qkv[:, channels:2 * channels], ('space', 'chan'), axis...]
    all_to_all x0 -> x1, starting transfers between devices: none -> 4.22 us  [all_by_exchange(): return jnp.concatenate(lax.all_to_all(sent, axis, 0, 0), axis=d)]
  transfers between devices with their start and end apart: 5 -> 6, of which waited for: 5 -> 5; matrix products, arithmetic and copies ran while one was open for 1% -> 3% of each run, Pallas kernels for 0% -> 0%
where the time goes in v1:
time: 139 us; the launch traced here: 138 us
  blocking collectives  35.3 us (25%)
  waiting for transfers between devices  30 us (22%)
  local copies, waits for them, and re-layouts  19.3 us (14%)
  starting transfers between devices  18.3 us (13%)
  between operations  13.6 us (10%)
  matrix products  12.7 us (9%)
  other arithmetic  8.46 us (6%)
    all_gather x1, blocking collectives, shards(): lax.all_gather(own_qkv[:, channels:2 * channels], ('space', 'chan'), axis...  19.9 us
    reduce_scatter x1, waiting for transfers between devices, shards(): lax.psum_scatter(partial_value, 'chan', scatter_dimension=1, tiled=True)  12.9 us
    concatenate x1, local copies, waits for them, and re-layouts, shards(): columns = jnp.concatenate(pieces, axis=1)  11.7 us
    ppermute x2, waiting for transfers between devices, passed_along(): return lax.ppermute(shard, axis, pairs)  9.56 us
    ppermute x2, starting transfers between devices, passed_along(): return lax.ppermute(shard, axis, pairs)  9.33 us
    dot_general x1, matrix products, shards(): jnp.dot(columns, flat_weight, preferred_element_type=jnp.float32)  8.41 us
    all_to_all x1, starting transfers between devices, all_by_exchange(): return jnp.concatenate(lax.all_to_all(sent, axis, 0, 0), axis=d)  4.22 us
    ppermute x1, waiting for transfers between devices, extended(): lax.ppermute(head, axis, [((i + 1) % count, i) for i in range(ends)])  4.13 us
  transfers between devices with their start and end apart: 6, of which 5 were waited for; matrix products, arithmetic and copies ran while one was open for 3% of the time, Pallas kernels for 0%

profile of v1, /device:TPU:0, one launch (start us, length us, event | category | flops | bytes accessed | tf_op | source)
XLA Modules:
  0.0 137.6 jit_solution(15959119249239768786)
XLA Ops:
  6.5 0.0 copy-start
  6.5 0.0 reduce-scatter.2.cloned.1.call-start
  6.5 1.2 fusion.13
  7.8 2.6 %psum.14 = f32[4,160]{1,0:T(4,128)S(1)} all-reduce(f32[4,160]{1,0:T(4,128)S(1)} %fusion.13), channel_id=1, replica_groups=mesh['groups'=2,'tm'=4,'space'=2,'chan'=2] {'chan'}, use_global_device_ids=true, to_apply=%region_1.0 | all-reduce | flops 640 | bytes 5120 | tf_op jit(solution)/shard_map/psum | solution.py:63
  10.4 1.3 multiply_convert_fusion.1
  11.7 5.8 %collective-permute-start = (bf16[4,160,192]{2,1,0:T(8,128)(2,1)S(1)}, bf16[4,160,192]{2,1,0:T(8,128)(2,1)S(1)}, u32[]{:S(2)}, u32[]{:S(2)}) collective-permute-start(bf16[4,160,192]{2,1,0:T(8,128)(2,1)S(1)} %multiply_convert_fusion.1), channel_id=1, source_target_pairs={{0,8},{4,12},{1,9},{5,13},{2,10},{6,14},{3,11},{7,15},{16,24},{20,... | collective-permute-start | bytes 737288 | tf_op jit(solution)/shard_map/ppermute | solution.py:18
  17.5 3.5 %collective-permute-start.1 = (bf16[4,160,192]{2,1,0:T(8,128)(2,1)S(1)}, bf16[4,160,192]{2,1,0:T(8,128)(2,1)S(1)}, u32[]{:S(2)}, u32[]{:S(2)}) collective-permute-start(bf16[4,160,192]{2,1,0:T(8,128)(2,1)S(1)} %multiply_convert_fusion.1), channel_id=1, source_target_pairs={{0,4},{4,8},{8,12},{1,5},{5,9},{9,13},{2,6},{6,10},{10,14},{3,7},{... | collective-permute-start | bytes 737288 | tf_op jit(solution)/shard_map/ppermute | solution.py:18
  21.0 1.3 multiply_convert_fusion
  22.3 3.3 %collective-permute-done = bf16[4,160,192]{2,1,0:T(8,128)(2,1)S(1)} collective-permute-done((bf16[4,160,192]{2,1,0:T(8,128)(2,1)S(1)}, bf16[4,160,192]{2,1,0:T(8,128)(2,1)S(1)}, u32[]{:S(2)}, u32[]{:S(2)}) %collective-permute-start) | collective-permute-done | bytes 245792 | tf_op jit(solution)/shard_map/ppermute | solution.py:18
  25.6 6.2 %collective-permute-done.1 = bf16[4,160,192]{2,1,0:T(8,128)(2,1)S(1)} collective-permute-done((bf16[4,160,192]{2,1,0:T(8,128)(2,1)S(1)}, bf16[4,160,192]{2,1,0:T(8,128)(2,1)S(1)}, u32[]{:S(2)}, u32[]{:S(2)}) %collective-permute-start.1) | collective-permute-done | bytes 245792 | tf_op jit(solution)/shard_map/ppermute | solution.py:18
  31.9 0.1 pad_maximum_fusion.12
  32.0 3.4 %collective-permute-start.2 = (bf16[3,1,160,192]{3,2,1,0:T(8,128)(2,1)S(1)}, bf16[3,1,160,192]{3,2,1,0:T(8,128)(2,1)S(1)}, u32[]{:S(2)}, u32[]{:S(2)}) collective-permute-start(bf16[3,1,160,192]{3,2,1,0:T(8,128)(2,1)S(1)} %get-tuple-element.31), channel_id=1, source_target_pairs={{0,2},{1,3},{4,6},{5,7},{8,10},{9,11},{12,14},{13,15},{16,18},{17,... | collective-permute-start | bytes 552968 | tf_op jit(solution)/shard_map/ppermute | solution.py:29
  35.4 1.3 collective-permute-start.3
  36.7 3.4 %collective-permute-done.2 = bf16[3,1,160,192]{3,2,1,0:T(8,128)(2,1)S(1)} collective-permute-done((bf16[3,1,160,192]{3,2,1,0:T(8,128)(2,1)S(1)}, bf16[3,1,160,192]{3,2,1,0:T(8,128)(2,1)S(1)}, u32[]{:S(2)}, u32[]{:S(2)}) %collective-permute-start.2) | collective-permute-done | bytes 184352 | tf_op jit(solution)/shard_map/ppermute | solution.py:29
  40.0 4.1 %collective-permute-done.3 = bf16[3,1,160,192]{3,2,1,0:T(8,128)(2,1)S(1)} collective-permute-done((bf16[3,1,160,192]{3,2,1,0:T(8,128)(2,1)S(1)}, bf16[3,1,160,192]{3,2,1,0:T(8,128)(2,1)S(1)}, u32[]{:S(2)}, u32[]{:S(2)}) %collective-permute-start.3) | collective-permute-done | bytes 184352 | tf_op jit(solution)/shard_map/ppermute | solution.py:31
  44.2 0.7 select_maximum_fusion
  44.9 2.3 %fusion.21 = (bf16[1,4,160,192]{3,2,1,0:T(8,128)(2,1)S(1)}, bf16[1,4,160,192]{3,2,1,0:T(8,128)(2,1)S(1)}, bf16[1,4,160,192]{3,2,1,0:T(8,128)(2,1)S(1)}, bf16[1,4...) fusion(bf16[3,6,162,192]{3,2,1,0:T(8,128)(2,1)S(1)} %select_max, ...), kind=kLoop, calls=%fused_computation.52 | loop fusion | bytes 8847360 | tf_op jit(solution)/shard_map/slice | solution.py:77
  47.3 1.0 pad_maximum_fusion
  48.3 1.0 pad_maximum_fusion.3
  49.3 11.7 %concatenate.19 = bf16[640,5184]{1,0:T(8,128)(2,1)} concatenate(bf16[640,192]{1,0:T(8,128)(2,1)} %bitcast.89, bf16[640,192]{1,0:T(8,128)(2,1)} %bitcast.94, bf16[640,192]{1,0:T(8,128)(2,1)} %bitcast.88, bf16[640,192]{1,0:T(8,128)(2,1)} %bitcast.87, bf16[640,192]{1,0:T(8,128)(2,1)S(1)} %bitcast.65, bf16[640,192]{1,0:T(8,128)(2,1)} %bitcast.86, bf16[640,192]{1,0:T(8,128)(2,1)} %bitcast.85, ...), dimensions={1} | concatenate | bytes 13271040 | tf_op jit(solution)/shard_map/concatenate | solution.py:81
  61.0 0.0 copy-start.1
  61.1 8.4 %fusion.24 = f32[640,384]{0,1:T(8,128)} fusion(bf16[640,5184]{1,0:T(8,128)(2,1)} %concatenate.19, bf16[5184,384]{1,0:T(8,128)(2,1)} %bitcast.98), kind=kOutput, calls=%fused_computation.55 | convolution fusion | flops 2548039680 | bytes 11599872 | tf_op jit(solution)/shard_map/dot_general | solution.py:83
  69.5 0.0 reduce-scatter.2.cloned.1.call-update
  69.5 0.0 copy-start.4
  69.5 0.2 copy.11
  69.7 0.8 copy-done.3
  70.5 2.4 %all_gather.6 = bf16[384,1152]{1,0:T(8,128)(2,1)S(1)} all-gather(bf16[192,1152]{1,0:T(8,128)(2,1)S(1)} %copy-done.3), channel_id=1, replica_groups=mesh['groups'=2,'tm'=4,'space'=2,'chan'=2] {'chan'}, dimensions={0}, use_global_device_ids=true | all-gather | bytes 1327104 | tf_op jit(solution)/shard_map/all_gather | solution.py:100
  72.9 12.9 %reduce-scatter.2.cloned.1.call-done = f32[640,192]{0,1:T(8,128)} async-done(((f32[640,384]{0,1:T(8,128)}), f32[640,192]{0,1:T(8,128)}) %reduce-scatter.2.cloned.1.call-update) | async-done | bytes 491536 | tf_op jit(solution)/shard_map/reduce_scatter | solution.py:84
  85.8 1.2 fusion.15
  87.0 2.5 %psum.15 = f32[640]{0:T(1024)S(1)} all-reduce(f32[640]{0:T(1024)S(1)} %get-tuple-element.5), channel_id=1, replica_groups=mesh['groups'=2,'tm'=4,'space'=2,'chan'=2] {'chan'}, use_global_device_ids=true, to_apply=%region_4.5 | all-reduce | flops 640 | bytes 5120 | tf_op jit(solution)/shard_map/psum | solution.py:90
  89.5 0.1 fusion.17
  89.6 0.3 all_to_all.27
  89.9 4.0 %all_to_all.37 = bf16[2,320,192]{1,2,0:T(8,128)(2,1)S(1)} all-to-all(bf16[2,320,192]{1,2,0:T(8,128)(2,1)S(1)} %copy.12), channel_id=1, replica_groups=mesh['groups'=2,'tm'=4,'space'=2,'chan'=2] {'chan'}, dimensions={0} | all-to-all | bytes 491520 | tf_op jit(solution)/shard_map/all_to_all | solution.py:99
  93.9 0.6 convolution_convert_fusion
  94.5 0.9 copy-done.2
  95.3 0.1 fusion.22
  95.4 1.1 stack.20
  96.5 4.2 %all-to-all-start.1 = ((bf16[4,320,384]{2,1,0:T(8,128)(2,1)}), bf16[4,320,384]{2,1,0:T(8,128)(2,1)}, u32[]{:S(2)}, u32[]{:S(2)}) async-start(bf16[4,320,384]{2,1,0:T(8,128)(2,1)} %stack.20), calls=%async_computation.2 | async-start | bytes 1966080 | tf_op jit(solution)/shard_map/all_to_all | solution.py:12
  100.7 19.9 %all_gather.7 = bf16[1280,384]{1,0:T(8,128)(2,1)S(1)} all-gather(bf16[320,384]{1,0:T(8,128)(2,1)S(1)} %get-tuple-element.33), channel_id=1, replica_groups=mesh['groups'=2,'tm'=4,'space'=2,'chan'=2] {'space','chan'}, dimensions={0}, use_global_device_ids=true | all-gather | bytes 1228800 | tf_op jit(solution)/shard_map/all_gather | solution.py:108
  120.5 1.7 %fusion.23 = (f32[320]{0:T(512)S(1)}, f32[320,1280]{1,0:T(8,128)S(1)}) fusion(bf16[1280,384]{1,0:T(8,128)(2,1)S(1)} %all_gather.7, bf16[320,1152]{1,0:T(8,128)(2,1)} %copy-done.2), kind=kOutput, calls=%fused_computation.54 | convolution fusion | flops 315391680 | bytes 2868480 | tf_op jit(solution)/shard_map/dot_general | solution.py:41
  122.2 0.4 fusion.6
  122.6 0.0 all-to-all-done.1
  122.6 2.1 %convolution_convert_fusion.1 = bf16[320,384]{1,0:T(8,128)(2,1)S(1)} fusion(bf16[384,384]{1,0:T(8,128)(2,1)S(1)} %copy-done, bf16[1280,384]{1,0:T(8,128)(2,1)} %bitcast.34, f32[320,1280]{1,0:T(8,128)S(1)} %get-tuple-element.36, f32[320]{0:T(512)S(1)} %broadcast_maximum_fusion, f32[320]{0:T(512)S(1)} %fusion.6), kind=kOutput, calls=%fused_computation.17 | convolution fusion | flops 410132480 | bytes 3164672 | tf_op jit(solution)/shard_map/dot_general | solution.py:113
  124.7 0.2 copy.13
  124.9 4.0 %all_to_all.38 = bf16[320,2,192]{0,2,1:T(8,128)(2,1)S(1)} all-to-all(bf16[320,2,192]{0,2,1:T(8,128)(2,1)S(1)} %bitcast.96), channel_id=1, replica_groups=mesh['groups'=2,'tm'=4,'space'=2,'chan'=2] {'chan'}, dimensions={1} | all-to-all | bytes 491520 | tf_op jit(solution)/shard_map/all_to_all | solution.py:116
  128.9 0.5 copy.14
  129.4 0.4 reshape.41
  129.8 0.9 copy.15
  (13 shorter events, 0.2 us)
Async XLA Ops:
  6.5 116.1 %copy-start = (bf16[384,384]{1,0:T(8,128)(2,1)S(1)}, bf16[384,384]{1,0:T(8,128)(2,1)}, u32[]{:S(2)}) copy-start(bf16[384,384]{1,0:T(8,128)(2,1)} %param.13) | copy-start | bytes 884740
  6.5 79.3 %reduce-scatter.2.cloned.1.call-start = ((), (), s32[]{:S(2)}) async-start(), calls=%async_computation.4 | async-start | bytes 1474560 | tf_op jit(solution)/shard_map/reduce_scatter | solution.py:84
  11.7 13.9 %collective-permute-start = (bf16[4,160,192]{2,1,0:T(8,128)(2,1)S(1)}, bf16[4,160,192]{2,1,0:T(8,128)(2,1)S(1)}, u32[]{:S(2)}, u32[]{:S(2)}) collective-permute-start(bf16[4,160,192]{2,1,0:T(8,128)(2,1)S(1)} %multiply_convert_fusion.1), channel_id=1, source_target_pairs={{0,8},{4,12},{1,9},{5,13},{2,10},{6,14},{3,11},{7,15},{16,24},{20,... | collective-permute-start | bytes 737288 | tf_op jit(solution)/shard_map/ppermute | solution.py:18
  17.5 14.3 %collective-permute-start.1 = (bf16[4,160,192]{2,1,0:T(8,128)(2,1)S(1)}, bf16[4,160,192]{2,1,0:T(8,128)(2,1)S(1)}, u32[]{:S(2)}, u32[]{:S(2)}) collective-permute-start(bf16[4,160,192]{2,1,0:T(8,128)(2,1)S(1)} %multiply_convert_fusion.1), channel_id=1, source_target_pairs={{0,4},{4,8},{8,12},{1,5},{5,9},{9,13},{2,6},{6,10},{10,14},{3,7},{... | collective-permute-start | bytes 737288 | tf_op jit(solution)/shard_map/ppermute | solution.py:18
  32.0 8.1 %collective-permute-start.2 = (bf16[3,1,160,192]{3,2,1,0:T(8,128)(2,1)S(1)}, bf16[3,1,160,192]{3,2,1,0:T(8,128)(2,1)S(1)}, u32[]{:S(2)}, u32[]{:S(2)}) collective-permute-start(bf16[3,1,160,192]{3,2,1,0:T(8,128)(2,1)S(1)} %get-tuple-element.31), channel_id=1, source_target_pairs={{0,2},{1,3},{4,6},{5,7},{8,10},{9,11},{12,14},{13,15},{16,18},{17,... | collective-permute-start | bytes 552968 | tf_op jit(solution)/shard_map/ppermute | solution.py:29
  35.4 8.8 %collective-permute-start.3 = (bf16[3,1,160,192]{3,2,1,0:T(8,128)(2,1)S(1)}, bf16[3,1,160,192]{3,2,1,0:T(8,128)(2,1)S(1)}, u32[]{:S(2)}, u32[]{:S(2)}) collective-permute-start(bf16[3,1,160,192]{3,2,1,0:T(8,128)(2,1)S(1)} %get-tuple-element.32), channel_id=1, source_target_pairs={{2,0},{3,1},{6,4},{7,5},{10,8},{11,9},{14,12},{15,13},{18,16},{19,... | collective-permute-start | bytes 552968 | tf_op jit(solution)/shard_map/ppermute | solution.py:31
  61.0 8.5 %copy-start.1 = (bf16[1,4,160,192]{3,2,1,0:T(8,128)(2,1)S(1)}, bf16[1,4,160,192]{3,2,1,0:T(8,128)(2,1)}, u32[]{:S(2)}) copy-start(bf16[1,4,160,192]{3,2,1,0:T(8,128)(2,1)} %param.7) | copy-start | bytes 737284
  69.5 1.0 copy-start.3
  69.5 16.4 %copy-start.5 = (f32[192]{0:T(256)S(1)}, f32[192]{0:T(256)}, u32[]{:S(2)}) copy-start(f32[192]{0:T(256)} %param.10) | copy-start | bytes 2308
  69.5 20.0 %copy-start.4 = (f32[192]{0:T(256)S(1)}, f32[192]{0:T(256)}, u32[]{:S(2)}) copy-start(f32[192]{0:T(256)} %param.11) | copy-start | bytes 2308
  94.5 0.9 copy-start.2
  96.5 26.2 %all-to-all-start.1 = ((bf16[4,320,384]{2,1,0:T(8,128)(2,1)}), bf16[4,320,384]{2,1,0:T(8,128)(2,1)}, u32[]{:S(2)}, u32[]{:S(2)}) async-start(bf16[4,320,384]{2,1,0:T(8,128)(2,1)} %stack.20), calls=%async_computation.2 | async-start | bytes 1966080 | tf_op jit(solution)/shard_map/all_to_all | solution.py:12
Sparse Core Ops, SparseCore 0:
  69.6 16.1 reduce-scatter.1
